TPU v7x, 32 devices: a whole 2x2x4 slice. The times are simulated.
32 devices in a mesh: freq: 4 (over x, core), grid: 8 (over z, y).
Axes of the slice: x: 2, y: 2, z: 4, core: 2. Of those that a mesh axis runs over, the one named last changes fastest.
Arguments:
- series: bfloat16 [128, 1024, 256], P('freq', 'grid'), may hold values from -8 to 8
- bins: int32 [4], replicated, may hold values from 32 to 127
- sensor_coords: int32 [3, 1024], replicated, may hold values from 0 to 63
- grid_coords: int32 [3, 2048], P(None, 'grid'), may hold values from 0 to 63
Outputs:
- bin_power: float32 [4, 2048], P('freq', 'grid')
- power: float32 [2048], P('grid')
All inputs are finite; a program needn't handle non-finite values.
Results may differ from a plain program's by a relative error of at most 0.0015.
Values may be sent and summed in bfloat16 or wider, within the bound.
No kernel may reach another device: no remote copies, remote signals or barrier semaphores. Data moves between devices by JAX's collectives and lax.ppermute only.
A program may use at most 64 MiB of HBM per device.

v0:
```python
import math
import jax
import jax.numpy as jnp
from jax import lax
from jax.sharding import PartitionSpec as P


def on_device(series, bins, sensor_coords, grid_coords):
    snap_local, channel_local, samples = series.shape
    all_bins = bins.shape[0]
    sample_index = jnp.arange(samples, dtype=jnp.int32)
    cycles = bins[:, None] * sample_index[None, :] % samples
    angles = 2.0 * math.pi / samples * cycles.astype(jnp.float32)
    scaling = (samples / 2.0) ** (-0.5)
    transform_table = jnp.stack([jnp.cos(angles) * scaling, -jnp.sin(angles) * scaling], 1)
    transform_table = transform_table.astype(jnp.bfloat16).reshape(2 * all_bins, samples)
    spectra = jnp.einsum("kt,sct->kcs", transform_table, series, preferred_element_type=jnp.float32)
    spectra = spectra.astype(jnp.bfloat16).reshape(all_bins, 2, channel_local, snap_local)
    regrouped = lax.all_to_all(spectra, "freq", split_axis=0, concat_axis=3, tiled=True)
    bin_count = regrouped.shape[0]
    snap_total = regrouped.shape[3]
    gathered = lax.all_gather(regrouped, "grid", axis=2, tiled=True)
    channels = gathered.shape[2]
    local_bins = lax.dynamic_slice_in_dim(bins, lax.axis_index("freq") * bin_count, bin_count)
    squared = jnp.zeros((grid_coords.shape[1], channels), jnp.int32)
    for axis_pos in range(3):
        offsets = grid_coords[axis_pos][:, None] - sensor_coords[axis_pos][None, :]
        squared = squared + offsets * offsets
    distance = jnp.sqrt(squared.astype(jnp.float32))
    phases = (
        4.0 * math.pi / samples * local_bins.astype(jnp.float32)[:, None, None] * distance[None]
    )
    amplitude = channels ** (-0.5)
    beam_real = (jnp.cos(phases) * amplitude).astype(jnp.bfloat16)
    beam_imag = (-jnp.sin(phases) * amplitude).astype(jnp.bfloat16)
    spec_real = gathered[:, 0]
    spec_imag = gathered[:, 1]

    def product(left, right):
        return jnp.einsum("fgc,fcs->fgs", left, right, preferred_element_type=jnp.float32)

    out_real = product(beam_real, spec_real) + product(beam_imag, spec_imag)
    out_imag = product(beam_real, spec_imag) - product(beam_imag, spec_real)
    bin_power = jnp.sum(out_real * out_real + out_imag * out_imag, 2) / snap_total
    summed = lax.psum(jnp.sum(bin_power, 0), "freq")
    power = summed / (bin_count * lax.axis_size("freq"))
    return (bin_power, power)


def solution(mesh):
    return jax.shard_map(
        on_device,
        mesh=mesh,
        in_specs=(P("freq", "grid", None), P(), P(), P(None, "grid")),
        out_specs=(P("freq", "grid"), P("grid")),
        check_vma=False,
    )
```

profile of v0, /device:TPU:0, one launch (start us, length us, event | category | flops | bytes accessed | tf_op | source)
XLA Modules:
  0.0 64.2 jit_solution(2394044324553024529)
XLA Ops:
  0.6 0.0 copy-start
  0.6 0.0 copy-start.4
  0.7 0.0 copy-start.1
  0.7 0.0 copy-start.3
  0.7 0.9 %multiply_convert_fusion.3 = (bf16[4,1,256]{2,0,1:T(4,128)(2,1)S(1)}, bf16[4,1,256]{2,0,1:T(4,128)(2,1)S(1)}) fusion(s32[4]{0:T(128)} %param.5), kind=kLoop, calls=%fused_computation.24 | loop fusion | flops 19456 | bytes 4112 | tf_op jit(solution)/shard_map/convert
  1.6 0.6 copy-done
  2.3 0.6 convolution_convert_fusion
  2.9 0.6 %copy.12 = bf16[4,2,128,32]{2,3,1,0:T(8,128)(2,1)} copy(bf16[4,2,128,32]{2,1,0,3:T(2,128)(2,1)S(1)} %bitcast.34) | data formatting | bytes 131072 | tf_op jit(solution)/shard_map/reshape | solution.py:18
  3.6 4.2 %all-to-all-start = ((bf16[4,2,128,32]{2,3,1,0:T(8,128)(2,1)}), bf16[4,2,128,32]{2,3,1,0:T(8,128)(2,1)S(1)}, u32[]{:S(2)}, u32[]{:S(2)}) async-start(bf16[4,2,128,32]{2,3,1,0:T(8,128)(2,1)} %copy.12), calls=%async_computation | async-start | bytes 131072 | tf_op jit(solution)/shard_map/all_to_all | solution.py:19
  7.8 0.0 copy-done.1
  7.8 0.0 copy-done.3
  7.8 0.0 copy-done.4
  7.9 0.6 dynamic_slice.3
  9.1 2.8 %all-to-all-done = bf16[4,2,128,32]{2,3,1,0:T(8,128)(2,1)S(1)} async-done(((bf16[4,2,128,32]{2,3,1,0:T(8,128)(2,1)}), bf16[4,2,128,32]{2,3,1,0:T(8,128)(2,1)S(1)}, u32[]{:S(2)}, u32[]{:S(2)}) %all-to-all-start) | async-done | bytes 65568 | tf_op jit(solution)/shard_map/all_to_all | solution.py:19
  11.9 28.8 %all_gather.3 = bf16[1,2,1024,128]{2,3,1,0:T(8,128)(2,1)S(1)} all-gather(bf16[1,2,128,128]{2,3,1,0:T(8,128)(2,1)S(1)} %bitcast.35), channel_id=1, replica_groups=mesh['freq'=4,'grid'=8] {'grid'}, dimensions={2}, use_global_device_ids=true | all-gather | bytes 589824 | tf_op jit(solution)/shard_map/all_gather | solution.py:22
  40.7 4.2 %fusion.8 = f32[256,128]{0,1:T(8,128)S(1)} fusion(s32[1024]{0:T(1024)S(1)} %bitcast.41, s32[256]{0:T(256)S(1)} %bitcast.53, s32[1024]{0:T(1024)S(1)} %bitcast.45, s32[256]{0:T(256)S(1)} %bitcast.57, s32[1024]{0:T(1024)S(1)} %bitcast.37, s32[256]{0:T(256)S(1)} %bitcast.49, f32[]{:T(128)} %bitcast, bf16[1,2,1024,128]{2,3,1,0:T(8,128)(2,1)S(1)} %all_gather.3), kind=kOutput, calls=%fused_computation.12 | convolution fusion | flops 70254592 | bytes 408580 | tf_op jit(solution)/shard_map/fgc,fcs->fgs/dot_general | solution.py:40
  44.9 4.2 %fusion.10 = f32[256,128]{0,1:T(8,128)S(1)} fusion(s32[1024]{0:T(1024)S(1)} %bitcast.42, s32[256]{0:T(256)S(1)} %bitcast.54, s32[1024]{0:T(1024)S(1)} %bitcast.46, s32[256]{0:T(256)S(1)} %bitcast.58, s32[1024]{0:T(1024)S(1)} %bitcast.38, s32[256]{0:T(256)S(1)} %bitcast.50, f32[]{:T(128)} %bitcast, bf16[1,2,1024,128]{2,3,1,0:T(8,128)(2,1)S(1)} %all_gather.3), kind=kOutput, calls=%fused_computation.13 | convolution fusion | flops 70254592 | bytes 408580 | tf_op jit(solution)/shard_map/fgc,fcs->fgs/dot_general | solution.py:40
  49.1 4.4 %fusion.2 = f32[256,128]{0,1:T(8,128)S(1)} fusion(f32[256,128]{0,1:T(8,128)S(1)} %fusion.10, s32[1024]{0:T(1024)S(1)} %bitcast.43, s32[256]{0:T(256)S(1)} %bitcast.55, s32[1024]{0:T(1024)S(1)} %bitcast.47, s32[256]{0:T(256)S(1)} %bitcast.59, s32[1024]{0:T(1024)S(1)} %bitcast.39, s32[256]{0:T(256)S(1)} %bitcast.51, f32[]{:T(128)} %bitcast, ...), kind=kOutput, calls=%fused_computation.4 | convolution fusion | flops 70582272 | bytes 539652 | tf_op jit(solution)/shard_map/fgc,fcs->fgs/dot_general | solution.py:40
  53.6 4.3 %fusion.3 = f32[256]{0:T(256)S(1)} fusion(f32[256,128]{0,1:T(8,128)S(1)} %fusion.2, f32[256,128]{0,1:T(8,128)S(1)} %fusion.8, s32[1024]{0:T(1024)S(1)} %bitcast.44, s32[256]{0:T(256)S(1)} %bitcast.56, s32[1024]{0:T(1024)S(1)} %bitcast.48, s32[256]{0:T(256)S(1)} %bitcast.60, s32[1024]{0:T(1024)S(1)} %bitcast.40, s32[256]{0:T(256)S(1)} %bitcast.52, f32[]{:T(128)} %bitcast, ...), kind=kOutput, calls=%fused_computation.6 | convolution fusion | flops 70647552 | bytes 540676 | tf_op jit(solution)/shard_map/fgc,fcs->fgs/dot_general | solution.py:40
  57.8 0.0 copy-start.2
  57.9 5.8 %psum.7 = f32[256]{0:T(256)S(1)} all-reduce(f32[256]{0:T(256)S(1)} %broadcast_multiply_fusion.1), channel_id=1, replica_groups=mesh['freq'=4,'grid'=8] {'freq'}, use_global_device_ids=true, to_apply=%region_1.2 | all-reduce | flops 256 | bytes 2048 | tf_op jit(solution)/shard_map/psum | solution.py:45
  63.6 0.6 broadcast_multiply_fusion
  64.2 0.0 copy-done.2
  (7 shorter events, 0.1 us)
Async XLA Ops:
  0.6 1.6 %copy-start = (bf16[32,128,256]{2,1,0:T(8,128)(2,1)S(1)}, bf16[32,128,256]{2,1,0:T(8,128)(2,1)}, u32[]{:S(2)}) copy-start(bf16[32,128,256]{2,1,0:T(8,128)(2,1)} %param.4) | copy-start | bytes 6291460
  0.6 7.2 %copy-start.4 = (s32[4]{0:T(128)S(1)}, s32[4]{0:T(128)}, u32[]{:S(2)}) copy-start(s32[4]{0:T(128)} %param.5) | copy-start | bytes 52
  0.7 7.1 %copy-start.1 = (s32[3,1024]{1,0:T(4,128)S(1)}, s32[3,1024]{1,0:T(4,128)}, u32[]{:S(2)}) copy-start(s32[3,1024]{1,0:T(4,128)} %param.6) | copy-start | bytes 36868
  0.7 7.2 %copy-start.3 = (s32[3,256]{1,0:T(4,128)S(1)}, s32[3,256]{1,0:T(4,128)}, u32[]{:S(2)}) copy-start(s32[3,256]{1,0:T(4,128)} %param.7) | copy-start | bytes 9220
  3.6 8.4 %all-to-all-start = ((bf16[4,2,128,32]{2,3,1,0:T(8,128)(2,1)}), bf16[4,2,128,32]{2,3,1,0:T(8,128)(2,1)S(1)}, u32[]{:S(2)}, u32[]{:S(2)}) async-start(bf16[4,2,128,32]{2,3,1,0:T(8,128)(2,1)} %copy.12), calls=%async_computation | async-start | bytes 131072 | tf_op jit(solution)/shard_map/all_to_all | solution.py:19
  57.8 6.3 %copy-start.2 = (f32[256]{0:T(256)}, f32[256]{0:T(256)S(1)}, u32[]{:S(2)}) copy-start(f32[256]{0:T(256)S(1)} %broadcast_multiply_fusion.1) | copy-start | bytes 3076
where the time goes:
time: 64.5 us; the launch traced here: 64.2 us
  blocking collectives  34.5 us (53%)
  matrix products  17.7 us (27%)
  starting transfers between devices  4.24 us (7%)
  waiting for transfers between devices  2.83 us (4%)
  local copies, waits for them, and re-layouts  1.93 us (3%)
  other arithmetic  1.51 us (2%)
  between operations  1.41 us (2%)
    all_gather x1, blocking collectives, on_device(): gathered = lax.all_gather(regrouped, 'grid', axis=2, tiled=True)  28.8 us
    dot_general x4, matrix products, product(): jnp.einsum('fgc,fcs->fgs', left, right, preferred_element_type=jnp.float32)  17.1 us
    psum x1, blocking collectives, on_device(): summed = lax.psum(jnp.sum(bin_power, 0), 'freq')  5.76 us
    all_to_all x1, starting transfers between devices, on_device(): lax.all_to_all(spectra, 'freq', split_axis=0, concat_axis=3, tiled=True)  4.24 us
    all_to_all x1, waiting for transfers between devices, on_device(): lax.all_to_all(spectra, 'freq', split_axis=0, concat_axis=3, tiled=True)  2.83 us
  transfers between devices with their start and end apart: 1, of which 1 were waited for; matrix products, arithmetic and copies ran while one was open for 1% of the time, Pallas kernels for 0%

commit v1 on v0

--- a/solution.py
+++ b/solution.py
@@ -19,7 +19,15 @@
     regrouped = lax.all_to_all(spectra, "freq", split_axis=0, concat_axis=3, tiled=True)
     bin_count = regrouped.shape[0]
     snap_total = regrouped.shape[3]
-    gathered = lax.all_gather(regrouped, "grid", axis=2, tiled=True)
+    ways, here, step = (lax.axis_size("grid"), lax.axis_index("grid"), regrouped.shape[2])
+    line, have = (regrouped, 1)
+    while have < ways:
+        line = jnp.concatenate(
+            [line, lax.ppermute(line, "grid", [(d, (d - have) % ways) for d in range(ways)])],
+            axis=2,
+        )
+        have = 2 * have
+    gathered = jnp.roll(line, here * step, axis=2)
     channels = gathered.shape[2]
     local_bins = lax.dynamic_slice_in_dim(bins, lax.axis_index("freq") * bin_count, bin_count)
     squared = jnp.zeros((grid_coords.shape[1], channels), jnp.int32)

time: 64.5 us -> 59.1 us (0.916)
  blocking collectives: 34.5 us -> 13.9 us
  waiting for transfers between devices: 2.83 us -> 16.1 us
  starting transfers between devices: 4.24 us -> 6.47 us
    all_gather x1 -> x0, blocking collectives: 28.8 us -> none  [on_device(): gathered = lax.all_gather(regrouped, 'grid', axis=2, tiled=True)]
    ppermute x0 -> x3, waiting for transfers between devices: none -> 16.1 us  [on_device(): lax.ppermute(line, 'grid', [(d, (d - have) % ways) for d in range(ways)])]
    all_to_all x0 -> x1, blocking collectives: none -> 8.16 us  [on_device(): lax.all_to_all(spectra, 'freq', split_axis=0, concat_axis=3, tiled=True)]
    ppermute x0 -> x3, starting transfers between devices: none -> 6.47 us  [on_device(): lax.ppermute(line, 'grid', [(d, (d - have) % ways) for d in range(ways)])]
    all_to_all x1 -> x0, starting transfers between devices: 4.24 us -> none  [on_device(): lax.all_to_all(spectra, 'freq', split_axis=0, concat_axis=3, tiled=True)]
    all_to_all x1 -> x0, waiting for transfers between devices: 2.83 us -> none  [on_device(): lax.all_to_all(spectra, 'freq', split_axis=0, concat_axis=3, tiled=True)]
  transfers between devices with their start and end apart: 1 -> 3, of which waited for: 1 -> 3; matrix products, arithmetic and copies ran while one was open for 1% -> 1% of each run, Pallas kernels for 0% -> 0%
where the time goes in v1:
time: 59.1 us; the launch traced here: 58.7 us
  matrix products  17.7 us (30%)
  waiting for transfers between devices  16.1 us (27%)
  blocking collectives  13.9 us (24%)
  starting transfers between devices  6.47 us (11%)
  other arithmetic  1.55 us (3%)
  between operations  1.49 us (3%)
  local copies, waits for them, and re-layouts  1.43 us (2%)
    dot_general x4, matrix products, product(): jnp.einsum('fgc,fcs->fgs', left, right, preferred_element_type=jnp.float32)  17.1 us
    ppermute x3, waiting for transfers between devices, on_device(): lax.ppermute(line, 'grid', [(d, (d - have) % ways) for d in range(ways)])  16.1 us
    all_to_all x1, blocking collectives, on_device(): lax.all_to_all(spectra, 'freq', split_axis=0, concat_axis=3, tiled=True)  8.16 us
    ppermute x3, starting transfers between devices, on_device(): lax.ppermute(line, 'grid', [(d, (d - have) % ways) for d in range(ways)])  6.47 us
    psum x1, blocking collectives, on_device(): summed = lax.psum(jnp.sum(bin_power, 0), 'freq')  5.76 us
  transfers between devices with their start and end apart: 3, of which 3 were waited for; matrix products, arithmetic and copies ran while one was open for 1% of the time, Pallas kernels for 0%

profile of v1, /device:TPU:0, one launch (start us, length us, event | category | flops | bytes accessed | tf_op | source)
XLA Modules:
  0.0 58.7 jit_solution(15893372353346681737)
XLA Ops:
  0.6 0.0 copy-start
  0.6 0.0 copy-start.4
  0.7 0.0 copy-start.1
  0.7 0.0 copy-start.3
  0.7 0.9 %multiply_convert_fusion.3 = (bf16[4,1,256]{2,0,1:T(4,128)(2,1)S(1)}, bf16[4,1,256]{2,0,1:T(4,128)(2,1)S(1)}) fusion(s32[4]{0:T(128)} %param.5), kind=kLoop, calls=%fused_computation.34 | loop fusion | flops 19456 | bytes 4112 | tf_op jit(solution)/shard_map/convert
  1.6 0.6 %copy-done = bf16[32,128,256]{2,1,0:T(8,128)(2,1)S(1)} copy-done((bf16[32,128,256]{2,1,0:T(8,128)(2,1)S(1)}, bf16[32,128,256]{2,1,0:T(8,128)(2,1)}, u32[]{:S(2)}) %copy-start) | copy-done | bytes 2097176
  2.3 0.6 %convolution_convert_fusion = bf16[8,32,128]{2,0,1:T(8,128)(2,1)S(1)} fusion(bf16[8,256,1]{1,0,2:T(8,128)(2,1)S(1)} %reshape.730, bf16[32,128,256]{2,1,0:T(8,128)(2,1)S(1)} %copy-done), kind=kOutput, calls=%fused_computation.5 | convolution fusion | flops 16809984 | bytes 2166784 | tf_op jit(solution)/shard_map/kt,sct->kcs/dot_general | solution.py:17
  2.9 8.2 %all_to_all.18 = bf16[4,2,128,32]{2,3,1,0:T(8,128)(2,1)S(1)} all-to-all(bf16[4,2,128,32]{2,3,1,0:T(8,128)(2,1)S(1)} %copy.12), channel_id=1, replica_groups=mesh['freq'=4,'grid'=8] {'freq'}, dimensions={0} | all-to-all | bytes 131072 | tf_op jit(solution)/shard_map/all_to_all | solution.py:19
  11.1 4.6 %collective-permute-start = (bf16[1,2,128,128]{2,3,1,0:T(8,128)(2,1)S(1)}, bf16[1,2,128,128]{2,3,1,0:T(8,128)(2,1)S(1)}, u32[]{:S(2)}, u32[]{:S(2)}) collective-permute-start(bf16[1,2,128,128]{2,3,1,0:T(8,128)(2,1)S(1)} %bitcast.34), channel_id=1, source_target_pairs={{0,7},{1,0},{2,1},{3,2},{4,3},{5,4},{6,5},{7,6},{8,15},{9,8},{10,9... | collective-permute-start | bytes 196616 | tf_op jit(solution)/shard_map/ppermute | solution.py:26
  15.7 0.0 copy-done.1
  15.7 0.0 copy-done.4
  15.7 0.6 dynamic_slice.7
  16.9 0.6 %collective-permute-done = bf16[1,2,128,128]{2,3,1,0:T(8,128)(2,1)S(1)} collective-permute-done((bf16[1,2,128,128]{2,3,1,0:T(8,128)(2,1)S(1)}, bf16[1,2,128,128]{2,3,1,0:T(8,128)(2,1)S(1)}, u32[]{:S(2)}, u32[]{:S(2)}) %collective-permute-start) | collective-permute-done | bytes 65568 | tf_op jit(solution)/shard_map/ppermute | solution.py:26
  17.6 1.5 %collective-permute-start.1 = (bf16[1,2,256,128]{2,3,1,0:T(8,128)(2,1)S(1)}, bf16[1,2,256,128]{2,3,1,0:T(8,128)(2,1)S(1)}, u32[]{:S(2)}, u32[]{:S(2)}) collective-permute-start(bf16[1,2,256,128]{2,3,1,0:T(8,128)(2,1)S(1)} %pad_maximum_fusion.1), channel_id=1, source_target_pairs={{0,6},{1,7},{2,0},{3,1},{4,2},{5,3},{6,4},{7,5},{8,14},{9,15},{10,... | collective-permute-start | bytes 393224 | tf_op jit(solution)/shard_map/ppermute | solution.py:26
  19.0 0.0 copy-done.3
  19.0 3.6 %collective-permute-done.1 = bf16[1,2,256,128]{2,3,1,0:T(8,128)(2,1)S(1)} collective-permute-done((bf16[1,2,256,128]{2,3,1,0:T(8,128)(2,1)S(1)}, bf16[1,2,256,128]{2,3,1,0:T(8,128)(2,1)S(1)}, u32[]{:S(2)}, u32[]{:S(2)}) %collective-permute-start.1) | collective-permute-done | bytes 131104 | tf_op jit(solution)/shard_map/ppermute | solution.py:26
  22.6 0.5 collective-permute-start.2
  23.1 11.9 %collective-permute-done.2 = bf16[1,2,512,128]{2,3,1,0:T(8,128)(2,1)S(1)} collective-permute-done((bf16[1,2,512,128]{2,3,1,0:T(8,128)(2,1)S(1)}, bf16[1,2,512,128]{2,3,1,0:T(8,128)(2,1)S(1)}, u32[]{:S(2)}, u32[]{:S(2)}) %collective-permute-start.2) | collective-permute-done | bytes 262176 | tf_op jit(solution)/shard_map/ppermute | solution.py:26
  35.2 4.2 %fusion.8 = f32[256,128]{0,1:T(8,128)S(1)} fusion(s32[1024]{0:T(1024)S(1)} %bitcast.45, s32[256]{0:T(256)S(1)} %bitcast.57, s32[1024]{0:T(1024)S(1)} %bitcast.49, s32[256]{0:T(256)S(1)} %bitcast.61, s32[1024]{0:T(1024)S(1)} %bitcast.41, s32[256]{0:T(256)S(1)} %bitcast.53, f32[]{:T(128)} %bitcast, ...), kind=kOutput, calls=%fused_computation.12 | convolution fusion | flops 70516736 | bytes 408584 | tf_op jit(solution)/shard_map/fgc,fcs->fgs/dot_general | solution.py:48
  39.5 4.2 %fusion.10 = f32[256,128]{0,1:T(8,128)S(1)} fusion(s32[1024]{0:T(1024)S(1)} %bitcast.46, s32[256]{0:T(256)S(1)} %bitcast.58, s32[1024]{0:T(1024)S(1)} %bitcast.50, s32[256]{0:T(256)S(1)} %bitcast.62, s32[1024]{0:T(1024)S(1)} %bitcast.42, s32[256]{0:T(256)S(1)} %bitcast.54, f32[]{:T(128)} %bitcast, ...), kind=kOutput, calls=%fused_computation.13 | convolution fusion | flops 70516736 | bytes 408588 | tf_op jit(solution)/shard_map/fgc,fcs->fgs/dot_general | solution.py:48
  43.7 4.4 %fusion.2 = f32[256,128]{0,1:T(8,128)S(1)} fusion(f32[256,128]{0,1:T(8,128)S(1)} %fusion.10, s32[1024]{0:T(1024)S(1)} %bitcast.47, s32[256]{0:T(256)S(1)} %bitcast.59, s32[1024]{0:T(1024)S(1)} %bitcast.51, s32[256]{0:T(256)S(1)} %bitcast.63, s32[1024]{0:T(1024)S(1)} %bitcast.43, s32[256]{0:T(256)S(1)} %bitcast.55, f32[]{:T(128)} %bitcast, ...), kind=kOutput, calls=%fused_computation.4 | convolution fusion | flops 70320128 | bytes 539656 | tf_op jit(solution)/shard_map/fgc,fcs->fgs/dot_general | solution.py:48
  48.1 4.2 %fusion.3 = f32[256]{0:T(256)S(1)} fusion(f32[256,128]{0,1:T(8,128)S(1)} %fusion.2, f32[256,128]{0,1:T(8,128)S(1)} %fusion.8, s32[1024]{0:T(1024)S(1)} %bitcast.48, s32[256]{0:T(256)S(1)} %bitcast.60, s32[1024]{0:T(1024)S(1)} %bitcast.52, s32[256]{0:T(256)S(1)} %bitcast.64, s32[1024]{0:T(1024)S(1)} %bitcast.44, s32[256]{0:T(256)S(1)} %bitcast.56, f32[]{:T(128)} %bitcast, ...), kind=kOutput, calls=%fused_computation.6 | convolution fusion | flops 70385408 | bytes 540684 | tf_op jit(solution)/shard_map/fgc,fcs->fgs/dot_general | solution.py:48
  52.3 0.0 copy-start.2
  52.4 5.8 %psum.7 = f32[256]{0:T(256)S(1)} all-reduce(f32[256]{0:T(256)S(1)} %broadcast_multiply_fusion.1), channel_id=1, replica_groups=mesh['freq'=4,'grid'=8] {'freq'}, use_global_device_ids=true, to_apply=%region_1.2 | all-reduce | flops 256 | bytes 2048 | tf_op jit(solution)/shard_map/psum | solution.py:53
  58.1 0.6 broadcast_multiply_fusion
  58.7 0.0 copy-done.2
  (18 shorter events, 0.3 us)
Async XLA Ops:
  0.6 1.6 %copy-start = (bf16[32,128,256]{2,1,0:T(8,128)(2,1)S(1)}, bf16[32,128,256]{2,1,0:T(8,128)(2,1)}, u32[]{:S(2)}) copy-start(bf16[32,128,256]{2,1,0:T(8,128)(2,1)} %param.4) | copy-start | bytes 6291460
  0.6 15.0 %copy-start.4 = (s32[4]{0:T(128)S(1)}, s32[4]{0:T(128)}, u32[]{:S(2)}) copy-start(s32[4]{0:T(128)} %param.5) | copy-start | bytes 52
  0.7 15.0 %copy-start.1 = (s32[3,1024]{1,0:T(4,128)S(1)}, s32[3,1024]{1,0:T(4,128)}, u32[]{:S(2)}) copy-start(s32[3,1024]{1,0:T(4,128)} %param.6) | copy-start | bytes 36868
  0.7 18.4 %copy-start.3 = (s32[3,256]{1,0:T(4,128)S(1)}, s32[3,256]{1,0:T(4,128)}, u32[]{:S(2)}) copy-start(s32[3,256]{1,0:T(4,128)} %param.7) | copy-start | bytes 9220
  11.1 6.5 %collective-permute-start = (bf16[1,2,128,128]{2,3,1,0:T(8,128)(2,1)S(1)}, bf16[1,2,128,128]{2,3,1,0:T(8,128)(2,1)S(1)}, u32[]{:S(2)}, u32[]{:S(2)}) collective-permute-start(bf16[1,2,128,128]{2,3,1,0:T(8,128)(2,1)S(1)} %bitcast.34), channel_id=1, source_target_pairs={{0,7},{1,0},{2,1},{3,2},{4,3},{5,4},{6,5},{7,6},{8,15},{9,8},{10,9... | collective-permute-start | bytes 196616 | tf_op jit(solution)/shard_map/ppermute | solution.py:26
  17.6 5.0 %collective-permute-start.1 = (bf16[1,2,256,128]{2,3,1,0:T(8,128)(2,1)S(1)}, bf16[1,2,256,128]{2,3,1,0:T(8,128)(2,1)S(1)}, u32[]{:S(2)}, u32[]{:S(2)}) collective-permute-start(bf16[1,2,256,128]{2,3,1,0:T(8,128)(2,1)S(1)} %pad_maximum_fusion.1), channel_id=1, source_target_pairs={{0,6},{1,7},{2,0},{3,1},{4,2},{5,3},{6,4},{7,5},{8,14},{9,15},{10,... | collective-permute-start | bytes 393224 | tf_op jit(solution)/shard_map/ppermute | solution.py:26
  22.6 12.4 %collective-permute-start.2 = (bf16[1,2,512,128]{2,3,1,0:T(8,128)(2,1)S(1)}, bf16[1,2,512,128]{2,3,1,0:T(8,128)(2,1)S(1)}, u32[]{:S(2)}, u32[]{:S(2)}) collective-permute-start(bf16[1,2,512,128]{2,3,1,0:T(8,128)(2,1)S(1)} %pad_maximum_fusion), channel_id=1, source_target_pairs={{0,4},{1,5},{2,6},{3,7},{4,0},{5,1},{6,2},{7,3},{8,12},{9,13},{10,... | collective-permute-start | bytes 786440 | tf_op jit(solution)/shard_map/ppermute | solution.py:26
  52.3 6.3 %copy-start.2 = (f32[256]{0:T(256)}, f32[256]{0:T(256)S(1)}, u32[]{:S(2)}) copy-start(f32[256]{0:T(256)S(1)} %broadcast_multiply_fusion.1) | copy-start | bytes 3076
